TPU v7x, 256 devices: a whole 4x4x8 slice. The times are simulated.
256 devices in a mesh: branch: 8 (over z), mp: 8 (over y_lo, x), dp: 4 (over y_hi, core).
Axes of the slice: x: 4, y: 4 (y_hi: 2, y_lo: 2; y = y_hi * 2 + y_lo), z: 8, core: 2. Of those that a mesh axis runs over, the one named last changes fastest.
Arguments:
- context: bfloat16 [4096, 4096], P(('branch', 'dp'), 'mp'), may hold values from -6 to 6
- residual: bfloat16 [4096, 4096], P(('branch', 'dp')), may hold values from -12 to 12
- attn_weight: bfloat16 [8, 4096, 4096], P('branch', 'mp', 'dp'), may hold values from -0.25 to 0.25
- norm_gain: bfloat16 [4096], replicated, may hold values from 0.099609375 to 1.8984375
- gate_weight: bfloat16 [8, 4096, 5504], P('branch', None, ('mp', 'dp')), may hold values from -0.09375 to 0.09375
- up_weight: bfloat16 [8, 4096, 5504], P('branch', None, ('mp', 'dp')), may hold values from -0.09375 to 0.09375
- down_weight: bfloat16 [8, 5504, 4096], P('branch', ('mp', 'dp')), may hold values from -0.078125 to 0.078125
- cotangent: bfloat16 [4096, 4096], P(('branch', 'dp')), may hold values from -0.796875 to 0.796875
- expert_ids: int32 [4096, 2], P(('branch', 'dp')), may hold values from 0 to 7, as said below
- gate_fixed: int32 [4096, 2], P(('branch', 'dp')), may hold values from 1 to 32767, as said below
Outputs:
- grad_gate: bfloat16 [8, 4096, 5504], P('branch', None, ('mp', 'dp'))
- grad_up: bfloat16 [8, 4096, 5504], P('branch', None, ('mp', 'dp'))
- grad_down: bfloat16 [8, 5504, 4096], P('branch', ('mp', 'dp'))
Inputs may be any that keep to these rules, and one draw needn't show every extreme that they name: `expert_ids`: the two entries of a row differ; in every aligned block of 128 rows some expert is named by more than 40 choices. `gate_fixed`: the two entries of a row sum to 32768.
All inputs are finite; a program needn't handle non-finite values.
Results may differ from a plain program's by a relative error of at most 0.025.
Values may be sent and summed in bfloat16 or wider, within the bound.
A program may use at most 128 MiB of HBM per device.

v0:
```python
import functools
import jax
import jax.numpy as jnp
from jax import lax
from jax.sharding import PartitionSpec as P


def slot_positions(id_block, capacity, experts):
    rows = id_block.shape[0]
    picks = jnp.concatenate([id_block[:, 0], id_block[:, 1]], axis=0)
    onehot = (picks[:, None] == jnp.arange(experts, dtype=jnp.int32)[None, :]).astype(jnp.int32)
    position = jnp.sum((jnp.cumsum(onehot, axis=0) - 1) * onehot, axis=1)
    position = jnp.where(position < capacity, position, -1)
    return jnp.stack([position[:rows], position[rows:]], axis=1)


def expert_pass(weight_set, totals, block_rows, first_row):
    w_gate, w_up, w_down = weight_set
    tokens_in, cotan_rows = block_rows
    pre_gate = jnp.dot(tokens_in, w_gate, preferred_element_type=jnp.float32)
    pre_up = jnp.dot(tokens_in, w_up, preferred_element_type=jnp.float32)
    sigmoid_gate = jax.nn.sigmoid(pre_gate)
    active = pre_gate * sigmoid_gate
    hidden = (active * pre_up).astype(jnp.bfloat16)
    back_grad = lax.dot_general(
        cotan_rows, w_down, (((1,), (1,)), ((), ())), preferred_element_type=jnp.float32
    )
    d_gate = (back_grad * pre_up * sigmoid_gate * (1.0 + pre_gate * (1.0 - sigmoid_gate))).astype(
        jnp.bfloat16
    )
    d_up = (back_grad * active).astype(jnp.bfloat16)
    contract = (((0,), (0,)), ((), ()))
    sum_gate = lax.dot_general(tokens_in, d_gate, contract, preferred_element_type=jnp.float32)
    sum_up = lax.dot_general(tokens_in, d_up, contract, preferred_element_type=jnp.float32)
    sum_down = lax.dot_general(hidden, cotan_rows, contract, preferred_element_type=jnp.float32)
    return (sum_gate, sum_up, sum_down)


def per_device(
    context,
    residual,
    attn_weight,
    norm_gain,
    gate_weight,
    up_weight,
    down_weight,
    cotangent,
    expert_ids,
    gate_fixed,
):
    branches = lax.axis_size("branch")
    summed = lax.psum(attn_weight[0].astype(jnp.float32).astype(jnp.bfloat16), "branch").astype(
        jnp.float32
    )
    merged = (summed / branches).astype(jnp.bfloat16)
    partial_out = jnp.dot(
        context,
        lax.all_gather(merged, "dp", axis=1, tiled=True),
        preferred_element_type=jnp.float32,
    ).astype(jnp.bfloat16)
    attention = lax.psum(partial_out.astype(jnp.float32).astype(jnp.bfloat16), "mp").astype(
        jnp.float32
    )
    mixed_in = residual.astype(jnp.float32) + attention
    inv_rms = lax.rsqrt(jnp.mean(mixed_in * mixed_in, axis=1, keepdims=True) + 1e-05)
    normed = (mixed_in * inv_rms * norm_gain.astype(jnp.float32)[None, :]).astype(jnp.bfloat16)
    model_width = residual.shape[1]
    group_tokens = residual.shape[0]
    experts = branches * gate_weight.shape[0]
    capacity = 5 * group_tokens // (2 * experts)
    slots = slot_positions(expert_ids, capacity, experts)
    slot_share = capacity // lax.axis_size("mp")
    offset = lax.axis_index("mp") * slot_share
    local_slot = slots - offset
    in_share = (slots >= 0) & (local_slot >= 0) & (local_slot < slot_share)
    slot_code = jnp.where(in_share, expert_ids * slot_share + local_slot, -1)
    target = jnp.arange(experts * slot_share, dtype=jnp.int32)
    matches = slot_code[None, :, :] == target[:, None, None]
    selector = jnp.any(matches, axis=2).astype(jnp.bfloat16)
    row_gate = jnp.sum(
        jnp.where(matches, gate_fixed[None, :, :].astype(jnp.float32) / 32768.0, 0.0), axis=(1, 2)
    )
    send_in = jnp.dot(selector, normed, preferred_element_type=jnp.float32).astype(jnp.bfloat16)
    send_in = send_in.reshape(experts, slot_share, model_width)
    cot_rows = jnp.dot(selector, cotangent, preferred_element_type=jnp.float32)
    send_cot = (
        (cot_rows * row_gate[:, None])
        .astype(jnp.bfloat16)
        .reshape(experts, slot_share, model_width)
    )
    hidden_width = gate_weight.shape[2]
    start_totals = (
        jnp.zeros((model_width, hidden_width), jnp.float32),
        jnp.zeros((model_width, hidden_width), jnp.float32),
        jnp.zeros((hidden_width, model_width), jnp.float32),
    )
    accumulate = functools.partial(expert_pass, (gate_weight[0], up_weight[0], down_weight[0]))
    routed_in, routed_cot = (
        lax.all_to_all(send_in, "branch", split_axis=0, concat_axis=1, tiled=True),
        lax.all_to_all(send_cot, "branch", split_axis=0, concat_axis=1, tiled=True),
    )
    totals = accumulate(
        start_totals,
        (
            lax.all_gather(routed_in[0], ("mp", "dp"), axis=0, tiled=True),
            lax.all_gather(routed_cot[0], ("mp", "dp"), axis=0, tiled=True),
        ),
        jnp.int32(0),
    )
    grad_gate = totals[0].astype(jnp.bfloat16)[None]
    grad_up = totals[1].astype(jnp.bfloat16)[None]
    grad_down = totals[2].astype(jnp.bfloat16)[None]
    return (grad_gate, grad_up, grad_down)


def solution(mesh):
    return jax.shard_map(
        per_device,
        mesh=mesh,
        in_specs=(
            P(("branch", "dp"), "mp"),
            P(("branch", "dp"), None),
            P("branch", "mp", "dp"),
            P(),
            P("branch", None, ("mp", "dp")),
            P("branch", None, ("mp", "dp")),
            P("branch", ("mp", "dp"), None),
            P(("branch", "dp"), None),
            P(("branch", "dp"), None),
            P(("branch", "dp"), None),
        ),
        out_specs=(
            P("branch", None, ("mp", "dp")),
            P("branch", None, ("mp", "dp")),
            P("branch", ("mp", "dp"), None),
        ),
        check_vma=False,
    )
```

profile of v0, /device:TPU:1, one launch (start us, length us, event | category | flops | bytes accessed | tf_op | source)
XLA Modules:
  0.0 354.2 jit_solution(13398183778796547387)
XLA Ops:
  8.0 0.0 copy-start
  8.0 0.0 all-reduce.3.cloned.1.call-start
  8.1 0.7 all-reduce.3.cloned.1.call-update
  8.7 0.0 all-gather.4.cloned.1.call-start
  8.8 77.8 %all-reduce.3.cloned.1.call-done = bf16[512,1024]{1,0:T(8,128)(2,1)} async-done(((bf16[512,1024]{1,0:T(8,128)(2,1)}), bf16[512,1024]{1,0:T(8,128)(2,1)}) %all-reduce.3.cloned.1.call-update) | async-done | bytes 1048592 | tf_op jit(solution)/shard_map/psum | solution.py:52
  86.6 2.4 multiply_convert_fusion.1
  89.0 0.0 all-gather.4.cloned.1.call-update
  89.0 0.0 all-reduce.5.cloned.1.call-start
  89.1 0.6 reduce-window.6
  89.7 0.2 slice_reduce_fusion
  90.0 0.1 fusion.18
  90.1 0.0 copy-start.2
  90.1 43.3 %all-gather.4.cloned.1.call-done = bf16[512,4096]{1,0:T(8,128)(2,1)} async-done(((bf16[512,1024]{1,0:T(8,128)(2,1)}), bf16[512,4096]{1,0:T(8,128)(2,1)}) %all-gather.4.cloned.1.call-update) | async-done | bytes 4194320 | tf_op jit(solution)/shard_map/all_gather | solution.py:58
  133.5 4.5 %fusion.3 = bf16[128,4096]{0,1:T(8,128)(2,1)} fusion(bf16[512,4096]{1,0:T(8,128)(2,1)} %all-gather.4.cloned.1.call-done, bf16[128,512]{1,0:T(8,128)(2,1)S(1)} %copy-done.4), kind=kOutput, calls=%fused_computation.7 | convolution fusion | flops 537395200 | bytes 5373952 | tf_op jit(solution)/shard_map/dot_general | solution.py:56
  138.0 0.0 all-reduce.5.cloned.1.call-update
  138.0 0.0 all-gather.8.cloned.1.call-start
  138.0 0.1 select_reduce_fusion
  138.2 0.0 copy-start.6
  138.2 0.3 fusion.4
  138.5 0.0 copy-start.3
  138.5 0.1 reshape.54
  138.6 24.0 %all_to_all.8 = bf16[8,5,4096]{2,1,0:T(8,128)(2,1)S(1)} all-to-all(bf16[8,5,4096]{2,1,0:T(8,128)(2,1)S(1)} %reshape.54), channel_id=1, replica_groups=mesh['branch'=8,'mp'=8,'dp'=4] {'branch'}, dimensions={0} | all-to-all | bytes 655360 | tf_op jit(solution)/shard_map/all_to_all | solution.py:100
  162.6 0.9 squeeze.28
  163.5 0.0 all-gather.8.cloned.1.call-update
  163.5 0.0 all-gather.6.cloned.1.call-start
  163.6 0.6 convert_element_type.69
  164.2 0.7 copy.19
  164.9 0.0 copy-start.5
  164.9 61.1 %all-reduce.5.cloned.1.call-done = bf16[128,4096]{0,1:T(8,128)(2,1)} async-done(((bf16[128,4096]{0,1:T(8,128)(2,1)}), bf16[128,4096]{0,1:T(8,128)(2,1)}) %all-reduce.5.cloned.1.call-update) | async-done | bytes 1048592 | tf_op jit(solution)/shard_map/psum | solution.py:61
  226.0 1.9 multiply_reduce_fusion
  227.9 1.0 convolution_convert_fusion.4
  228.9 0.1 reshape.53
  229.1 21.5 %all_to_all.9 = bf16[8,5,4096]{2,1,0:T(8,128)(2,1)S(1)} all-to-all(bf16[8,5,4096]{2,1,0:T(8,128)(2,1)S(1)} %reshape.53), channel_id=1, replica_groups=mesh['branch'=8,'mp'=8,'dp'=4] {'branch'}, dimensions={0} | all-to-all | bytes 655360 | tf_op jit(solution)/shard_map/all_to_all | solution.py:99
  250.5 0.9 squeeze.27
  251.4 0.0 all-gather.6.cloned.1.call-update
  251.4 0.0 copy-start.9
  251.4 0.0 all-gather.8.cloned.1.call-done
  251.5 8.6 %fusion.9 = f32[1280,172]{0,1:T(8,128)} fusion(bf16[1280,4096]{1,0:T(8,128)(2,1)} %all-gather.8.cloned.1.call-done, bf16[1,172,4096]{2,1,0:T(8,128)(2,1)S(1)} %copy-done), kind=kOutput, calls=%fused_computation.19 | convolution fusion | flops 1803550720 | bytes 12775424 | tf_op jit(solution)/shard_map/dot_general | solution.py:25
  260.1 61.2 %all-gather.6.cloned.1.call-done = bf16[1280,4096]{1,0:T(8,128)(2,1)} async-done(((bf16[40,4096]{1,0:T(8,128)(2,1)}), bf16[1280,4096]{1,0:T(8,128)(2,1)}) %all-gather.6.cloned.1.call-update) | async-done | bytes 10485776 | tf_op jit(solution)/shard_map/all_gather | solution.py:105
  321.3 7.8 %fusion.5 = f32[1280,172]{0,1:T(8,128)S(1)} fusion(bf16[1280,4096]{1,0:T(8,128)(2,1)} %all-gather.6.cloned.1.call-done, bf16[1,4096,172]{1,2,0:T(8,128)(2,1)S(1)} %copy-done.9), kind=kOutput, calls=%fused_computation.15 | convolution fusion | flops 1803550720 | bytes 12775424 | tf_op jit(solution)/shard_map/dot_general | solution.py:20
  329.1 0.0 slice-start.2
  329.1 0.0 slice-start.3
  329.1 0.0 slice-start.4
  329.1 7.8 %fusion.7 = f32[1280,172]{0,1:T(8,128)S(1)} fusion(bf16[1280,4096]{1,0:T(8,128)(2,1)} %all-gather.6.cloned.1.call-done, bf16[1,4096,172]{1,2,0:T(8,128)(2,1)S(1)} %copy-done.10), kind=kOutput, calls=%fused_computation.17 | convolution fusion | flops 1803550720 | bytes 12775424 | tf_op jit(solution)/shard_map/dot_general | solution.py:21
  336.9 0.0 copy-start.11
  336.9 3.2 fusion.2
  340.2 3.5 fusion
  343.7 3.3 fusion.1
  (39 shorter events, 0.2 us)
Async XLA Ops:
  8.0 243.5 %copy-start = (bf16[1,172,4096]{2,1,0:T(8,128)(2,1)S(1)}, bf16[1,172,4096]{2,1,0:T(8,128)(2,1)}, u32[]{:S(2)}) copy-start(bf16[1,172,4096]{2,1,0:T(8,128)(2,1)} %param.16) | copy-start | bytes 4227076
  8.0 78.6 %all-reduce.3.cloned.1.call-start = ((), (), s32[]{:S(2)}) async-start(), calls=%async_computation.2 | async-start | bytes 2097152 | tf_op jit(solution)/shard_map/psum | solution.py:52
  8.1 81.0 %copy-start.7 = (s32[128,2]{0,1:T(2,128)S(1)}, s32[128,2]{0,1:T(2,128)}, u32[]{:S(2)}) copy-start(s32[128,2]{0,1:T(2,128)} %param.18) | copy-start | bytes 3076
  8.1 82.0 %copy-start.8 = (s32[128,2]{0,1:T(2,128)S(1)}, s32[128,2]{0,1:T(2,128)}, u32[]{:S(2)}) copy-start(s32[128,2]{0,1:T(2,128)} %param.19) | copy-start | bytes 3076
  8.1 125.4 %copy-start.4 = (bf16[128,512]{1,0:T(8,128)(2,1)S(1)}, bf16[128,512]{1,0:T(8,128)(2,1)}, u32[]{:S(2)}) copy-start(bf16[128,512]{1,0:T(8,128)(2,1)} %param.10) | copy-start | bytes 393220
  8.7 124.7 %all-gather.4.cloned.1.call-start = ((), (), s32[]{:S(2)}) async-start(), calls=%async_computation.3 | async-start | bytes 5242880 | tf_op jit(solution)/shard_map/all_gather | solution.py:58
  89.0 137.0 %all-reduce.5.cloned.1.call-start = ((), (), s32[]{:S(2)}) async-start(), calls=%async_computation.4 | async-start | bytes 2097152 | tf_op jit(solution)/shard_map/psum | solution.py:61
  90.1 48.0 %copy-start.2 = (bf16[128,4096]{1,0:T(8,128)(2,1)S(1)}, bf16[128,4096]{1,0:T(8,128)(2,1)}, u32[]{:S(2)}) copy-start(bf16[128,4096]{1,0:T(8,128)(2,1)} %param.17) | copy-start | bytes 3145732
  138.0 113.5 %all-gather.8.cloned.1.call-start = ((), (), s32[]{:S(2)}) async-start(), calls=%async_computation.6 | async-start | bytes 10813440 | tf_op jit(solution)/shard_map/all_gather | solution.py:106
  138.2 25.4 %copy-start.6 = (bf16[4096]{0:T(1024)(128)(2,1)S(1)}, bf16[4096]{0:T(1024)(128)(2,1)}, u32[]{:S(2)}) copy-start(bf16[4096]{0:T(1024)(128)(2,1)} %param.13) | copy-start | bytes 24580
  138.5 25.7 %copy-start.3 = (bf16[128,4096]{1,0:T(8,128)(2,1)S(1)}, bf16[128,4096]{1,0:T(8,128)(2,1)}, u32[]{:S(2)}) copy-start(bf16[128,4096]{1,0:T(8,128)(2,1)} %param.11) | copy-start | bytes 3145732
  163.5 157.8 %all-gather.6.cloned.1.call-start = ((), (), s32[]{:S(2)}) async-start(), calls=%async_computation.5 | async-start | bytes 10813440 | tf_op jit(solution)/shard_map/all_gather | solution.py:105
  164.9 63.0 %copy-start.5 = (f32[4096]{0:T(1024)S(1)}, f32[4096]{0:T(1024)}, u32[]{:S(2)}) copy-start(f32[4096]{0:T(1024)} %convert_element_type.69) | copy-start | bytes 49156
  226.0 1.9 copy-start.1
  251.4 69.9 %copy-start.9 = (bf16[1,4096,172]{1,2,0:T(8,128)(2,1)S(1)}, bf16[1,4096,172]{1,2,0:T(8,128)(2,1)}, u32[]{:S(2)}) copy-start(bf16[1,4096,172]{1,2,0:T(8,128)(2,1)} %param.14) | copy-start | bytes 4227076
  321.3 7.8 %copy-start.10 = (bf16[1,4096,172]{1,2,0:T(8,128)(2,1)S(1)}, bf16[1,4096,172]{1,2,0:T(8,128)(2,1)}, u32[]{:S(2)}) copy-start(bf16[1,4096,172]{1,2,0:T(8,128)(2,1)} %param.15) | copy-start | bytes 4227076
  321.3 15.6 %slice-start = ((s8[10485760]{0:T(1024)(128)(4,1)}), s8[4194304]{0:T(1024)(128)(4,1)S(1)}, s32[]{:S(2)}) async-start(s8[10485760]{0:T(1024)(128)(4,1)} %bitcast.46), calls=%async_computation.7 | async-start | bytes 8388608
  321.3 15.6 %slice-start.1 = ((s8[10485760]{0:T(1024)(128)(4,1)}), s8[4194304]{0:T(1024)(128)(4,1)S(1)}, s32[]{:S(2)}) async-start(s8[10485760]{0:T(1024)(128)(4,1)} %bitcast.46), calls=%async_computation.8 | async-start | bytes 8388608
  329.1 7.8 %slice-start.2 = ((s8[10485760]{0:T(1024)(128)(4,1)}), s8[2097152]{0:T(1024)(128)(4,1)S(1)}, s32[]{:S(2)}) async-start(s8[10485760]{0:T(1024)(128)(4,1)} %bitcast.46), calls=%async_computation.9 | async-start | bytes 4194304
  329.1 11.1 %slice-start.3 = ((s8[10485760]{0:T(1024)(128)(4,1)}), s8[4194304]{0:T(1024)(128)(4,1)S(1)}, s32[]{:S(2)}) async-start(s8[10485760]{0:T(1024)(128)(4,1)} %bitcast.48), calls=%async_computation.10 | async-start | bytes 8388608
  329.1 11.1 %slice-start.4 = ((s8[10485760]{0:T(1024)(128)(4,1)}), s8[4194304]{0:T(1024)(128)(4,1)S(1)}, s32[]{:S(2)}) async-start(s8[10485760]{0:T(1024)(128)(4,1)} %bitcast.48), calls=%async_computation.11 | async-start | bytes 8388608
  336.9 3.3 slice-start.5
  336.9 3.3 copy-start.11
Sparse Core Ops, SparseCore 0:
  11.2 75.3 all-reduce.2
  89.1 44.2 all-gather.3
  138.1 87.8 all-reduce.4
Sparse Core Ops, SparseCore 1:
  163.6 76.4 all-gather.7
  251.5 69.8 all-gather.5
where the time goes:
time: 354 us
  waiting for transfers between devices  244 us (69%)
  blocking collectives  45.5 us (13%)
  matrix products  40 us (11%)
  between operations  15.5 us (4%)
  other arithmetic  5.78 us (2%)
    psum x1, waiting for transfers between devices, per_device(): lax.psum(attn_weight[0].astype(jnp.float32).astype(jnp.bfloat16), 'branch')  77.8 us
    all_gather x1, waiting for transfers between devices, per_device(): lax.all_gather(routed_in[0], ('mp', 'dp'), axis=0, tiled=True)  61.2 us
    psum x1, waiting for transfers between devices, per_device(): lax.psum(partial_out.astype(jnp.float32).astype(jnp.bfloat16), 'mp')  61.1 us
    all_gather x1, waiting for transfers between devices, per_device(): lax.all_gather(merged, 'dp', axis=1, tiled=True)  43.3 us
    all_to_all x1, blocking collectives, per_device(): lax.all_to_all(send_cot, 'branch', split_axis=0, concat_axis=1, tiled=True)  24 us
    all_to_all x1, blocking collectives, per_device(): lax.all_to_all(send_in, 'branch', split_axis=0, concat_axis=1, tiled=True)  21.5 us
    dot_general x1, matrix products, expert_pass(): lax.dot_general(cotan_rows, w_down, (((1,), (1,)), ((), ())), preferred_e...  8.63 us
    dot_general x1, matrix products, expert_pass(): pre_gate = jnp.dot(tokens_in, w_gate, preferred_element_type=jnp.float32)  7.76 us
  transfers between devices with their start and end apart: 5, of which 4 were waited for; matrix products, arithmetic and copies ran while one was open for 5% of the time, Pallas kernels for 0%

commit v1 on v0

--- a/solution.py
+++ b/solution.py
@@ -55,7 +55,7 @@
     merged = (summed / branches).astype(jnp.bfloat16)
     partial_out = jnp.dot(
         context,
-        lax.all_gather(merged, "dp", axis=1, tiled=True),
+        jnp.concatenate(lax.all_gather(merged, "dp"), axis=1),
         preferred_element_type=jnp.float32,
     ).astype(jnp.bfloat16)
     attention = lax.psum(partial_out.astype(jnp.float32).astype(jnp.bfloat16), "mp").astype(

time: 354 us -> 360 us (1.017)
  local copies, waits for them, and re-layouts: 2.98 us -> 9.24 us
    reshape x0 -> x1, local copies, waits for them, and re-layouts: none -> 6.26 us  [per_device(): jnp.concatenate(lax.all_gather(merged, 'dp'), axis=1)]
  transfers between devices with their start and end apart: 5 -> 5, of which waited for: 4 -> 4; matrix products, arithmetic and copies ran while one was open for 5% -> 4% of each run, Pallas kernels for 0% -> 0%
where the time goes in v1:
time: 360 us; the launch traced here: 359 us
  waiting for transfers between devices  243 us (68%)
  blocking collectives  45.6 us (13%)
  matrix products  40 us (11%)
  between operations  15.5 us (4%)
  local copies, waits for them, and re-layouts  9.24 us (3%)
  other arithmetic  5.77 us (2%)
    psum x1, waiting for transfers between devices, per_device(): lax.psum(attn_weight[0].astype(jnp.float32).astype(jnp.bfloat16), 'branch')  77.8 us
    all_gather x1, waiting for transfers between devices, per_device(): lax.all_gather(routed_in[0], ('mp', 'dp'), axis=0, tiled=True)  61 us
    psum x1, waiting for transfers between devices, per_device(): lax.psum(partial_out.astype(jnp.float32).astype(jnp.bfloat16), 'mp')  60.2 us
    all_gather x1, waiting for transfers between devices, per_device(): lax.all_gather(merged, 'dp')  43.4 us
    all_to_all x1, blocking collectives, per_device(): lax.all_to_all(send_cot, 'branch', split_axis=0, concat_axis=1, tiled=True)  24 us
    all_to_all x1, blocking collectives, per_device(): lax.all_to_all(send_in, 'branch', split_axis=0, concat_axis=1, tiled=True)  21.5 us
    dot_general x1, matrix products, expert_pass(): lax.dot_general(cotan_rows, w_down, (((1,), (1,)), ((), ())), preferred_e...  8.63 us
    dot_general x1, matrix products, expert_pass(): pre_up = jnp.dot(tokens_in, w_up, preferred_element_type=jnp.float32)  7.75 us
  transfers between devices with their start and end apart: 5, of which 4 were waited for; matrix products, arithmetic and copies ran while one was open for 4% of the time, Pallas kernels for 0%

profile of v1, /device:TPU:1, one launch (start us, length us, event | category | flops | bytes accessed | tf_op | source)
XLA Modules:
  0.0 359.3 jit_solution(9765528886275625171)
XLA Ops:
  8.0 0.0 copy-start
  8.0 0.0 all-reduce.3.cloned.1.call-start
  8.1 0.7 all-reduce.3.cloned.1.call-update
  8.7 0.0 all-gather.9.cloned.1.call-start
  8.8 77.8 %all-reduce.3.cloned.1.call-done = bf16[512,1024]{1,0:T(8,128)(2,1)} async-done(((bf16[512,1024]{1,0:T(8,128)(2,1)}), bf16[512,1024]{1,0:T(8,128)(2,1)}) %all-reduce.3.cloned.1.call-update) | async-done | bytes 1048592 | tf_op jit(solution)/shard_map/psum | solution.py:52
  86.6 2.4 multiply_convert_fusion.1
  89.0 0.0 all-gather.9.cloned.1.call-update
  89.0 0.0 all-reduce.5.cloned.1.call-start
  89.1 0.6 reduce-window.6
  89.7 0.2 slice_reduce_fusion
  90.0 0.1 fusion.18
  90.1 43.4 %all-gather.9.cloned.1.call-done = bf16[2048,1024]{1,0:T(8,128)(2,1)} async-done(((bf16[512,1024]{1,0:T(8,128)(2,1)}), bf16[2048,1024]{1,0:T(8,128)(2,1)}) %all-gather.9.cloned.1.call-update) | async-done | bytes 4194320 | tf_op jit(solution)/shard_map/all_gather | solution.py:58
  133.5 6.3 %copy.24 = bf16[512,4,1024]{0,2,1:T(8,128)(2,1)} copy(bf16[512,4,1024]{2,0,1:T(8,128)(2,1)} %bitcast.50) | data formatting | bytes 8388608 | tf_op jit(solution)/shard_map/reshape | solution.py:58
  139.7 4.5 %fusion.3 = bf16[128,4096]{0,1:T(8,128)(2,1)} fusion(bf16[512,4096]{0,1:T(8,128)(2,1)} %bitcast.49, bf16[128,512]{1,0:T(8,128)(2,1)S(1)} %copy-done.4), kind=kOutput, calls=%fused_computation.7 | convolution fusion | flops 537395200 | bytes 5373952 | tf_op jit(solution)/shard_map/dot_general | solution.py:56
  144.2 0.0 all-reduce.5.cloned.1.call-update
  144.3 0.0 all-gather.7.cloned.1.call-start
  144.3 0.1 select_reduce_fusion
  144.5 0.0 copy-start.6
  144.5 0.3 fusion.4
  144.7 0.0 copy-start.3
  144.8 0.1 reshape.62
  144.9 24.0 %all_to_all.8 = bf16[8,5,4096]{2,1,0:T(8,128)(2,1)S(1)} all-to-all(bf16[8,5,4096]{2,1,0:T(8,128)(2,1)S(1)} %reshape.62), channel_id=1, replica_groups=mesh['branch'=8,'mp'=8,'dp'=4] {'branch'}, dimensions={0} | all-to-all | bytes 655360 | tf_op jit(solution)/shard_map/all_to_all | solution.py:100
  169.0 0.9 squeeze.28
  169.8 0.0 all-gather.7.cloned.1.call-update
  169.8 0.0 all-gather.5.cloned.1.call-start
  169.9 0.6 convert_element_type.69
  170.5 0.7 copy.23
  171.2 0.0 copy-start.5
  171.2 60.2 %all-reduce.5.cloned.1.call-done = bf16[128,4096]{0,1:T(8,128)(2,1)} async-done(((bf16[128,4096]{0,1:T(8,128)(2,1)}), bf16[128,4096]{0,1:T(8,128)(2,1)}) %all-reduce.5.cloned.1.call-update) | async-done | bytes 1048592 | tf_op jit(solution)/shard_map/psum | solution.py:61
  231.3 1.9 multiply_reduce_fusion
  233.2 1.0 convolution_convert_fusion.4
  234.3 0.1 reshape.61
  234.4 21.5 %all_to_all.9 = bf16[8,5,4096]{2,1,0:T(8,128)(2,1)S(1)} all-to-all(bf16[8,5,4096]{2,1,0:T(8,128)(2,1)S(1)} %reshape.61), channel_id=1, replica_groups=mesh['branch'=8,'mp'=8,'dp'=4] {'branch'}, dimensions={0} | all-to-all | bytes 655360 | tf_op jit(solution)/shard_map/all_to_all | solution.py:99
  255.9 0.9 squeeze.27
  256.8 0.0 all-gather.5.cloned.1.call-update
  256.8 0.0 copy-start.9
  256.8 0.0 all-gather.7.cloned.1.call-done
  256.9 8.6 %fusion.9 = f32[1280,172]{0,1:T(8,128)} fusion(bf16[1280,4096]{1,0:T(8,128)(2,1)} %all-gather.7.cloned.1.call-done, bf16[1,172,4096]{2,1,0:T(8,128)(2,1)S(1)} %copy-done), kind=kOutput, calls=%fused_computation.19 | convolution fusion | flops 1803550720 | bytes 12775424 | tf_op jit(solution)/shard_map/dot_general | solution.py:25
  265.5 61.0 %all-gather.5.cloned.1.call-done = bf16[1280,4096]{1,0:T(8,128)(2,1)} async-done(((bf16[40,4096]{1,0:T(8,128)(2,1)}), bf16[1280,4096]{1,0:T(8,128)(2,1)}) %all-gather.5.cloned.1.call-update) | async-done | bytes 10485776 | tf_op jit(solution)/shard_map/all_gather | solution.py:105
  326.5 7.8 %fusion.5 = f32[1280,172]{0,1:T(8,128)S(1)} fusion(bf16[1280,4096]{1,0:T(8,128)(2,1)} %all-gather.5.cloned.1.call-done, bf16[1,4096,172]{1,2,0:T(8,128)(2,1)S(1)} %copy-done.9), kind=kOutput, calls=%fused_computation.15 | convolution fusion | flops 1803550720 | bytes 12775424 | tf_op jit(solution)/shard_map/dot_general | solution.py:20
  334.2 0.0 slice-start.3
  334.3 0.0 slice-start.4
  334.3 7.8 %fusion.7 = f32[1280,172]{0,1:T(8,128)S(1)} fusion(bf16[1280,4096]{1,0:T(8,128)(2,1)} %all-gather.5.cloned.1.call-done, bf16[1,4096,172]{1,2,0:T(8,128)(2,1)S(1)} %copy-done.10), kind=kOutput, calls=%fused_computation.17 | convolution fusion | flops 1803550720 | bytes 12775424 | tf_op jit(solution)/shard_map/dot_general | solution.py:21
  342.1 0.0 slice-start.5
  342.1 0.0 copy-start.11
  342.1 3.3 fusion.2
  345.4 3.5 fusion
  348.9 3.3 fusion.1
  (40 shorter events, 0.2 us)
Async XLA Ops:
  8.0 248.9 %copy-start = (bf16[1,172,4096]{2,1,0:T(8,128)(2,1)S(1)}, bf16[1,172,4096]{2,1,0:T(8,128)(2,1)}, u32[]{:S(2)}) copy-start(bf16[1,172,4096]{2,1,0:T(8,128)(2,1)} %param.16) | copy-start | bytes 4227076
  8.0 78.6 %all-reduce.3.cloned.1.call-start = ((), (), s32[]{:S(2)}) async-start(), calls=%async_computation.2 | async-start | bytes 2097152 | tf_op jit(solution)/shard_map/psum | solution.py:52
  8.1 81.0 %copy-start.7 = (s32[128,2]{0,1:T(2,128)S(1)}, s32[128,2]{0,1:T(2,128)}, u32[]{:S(2)}) copy-start(s32[128,2]{0,1:T(2,128)} %param.18) | copy-start | bytes 3076
  8.1 82.0 %copy-start.8 = (s32[128,2]{0,1:T(2,128)S(1)}, s32[128,2]{0,1:T(2,128)}, u32[]{:S(2)}) copy-start(s32[128,2]{0,1:T(2,128)} %param.19) | copy-start | bytes 3076
  8.7 124.7 %all-gather.9.cloned.1.call-start = ((), (), s32[]{:S(2)}) async-start(), calls=%async_computation.6 | async-start | bytes 5242880 | tf_op jit(solution)/shard_map/all_gather | solution.py:58
  89.0 142.3 %all-reduce.5.cloned.1.call-start = ((), (), s32[]{:S(2)}) async-start(), calls=%async_computation.3 | async-start | bytes 2097152 | tf_op jit(solution)/shard_map/psum | solution.py:61
  133.5 6.3 %copy-start.4 = (bf16[128,512]{1,0:T(8,128)(2,1)S(1)}, bf16[128,512]{1,0:T(8,128)(2,1)}, u32[]{:S(2)}) copy-start(bf16[128,512]{1,0:T(8,128)(2,1)} %param.10) | copy-start | bytes 393220
  139.7 4.7 %copy-start.2 = (bf16[128,4096]{1,0:T(8,128)(2,1)S(1)}, bf16[128,4096]{1,0:T(8,128)(2,1)}, u32[]{:S(2)}) copy-start(bf16[128,4096]{1,0:T(8,128)(2,1)} %param.17) | copy-start | bytes 3145732
  144.3 112.6 %all-gather.7.cloned.1.call-start = ((), (), s32[]{:S(2)}) async-start(), calls=%async_computation.5 | async-start | bytes 10813440 | tf_op jit(solution)/shard_map/all_gather | solution.py:106
  144.5 25.4 %copy-start.6 = (bf16[4096]{0:T(1024)(128)(2,1)S(1)}, bf16[4096]{0:T(1024)(128)(2,1)}, u32[]{:S(2)}) copy-start(bf16[4096]{0:T(1024)(128)(2,1)} %param.13) | copy-start | bytes 24580
  144.7 25.8 %copy-start.3 = (bf16[128,4096]{1,0:T(8,128)(2,1)S(1)}, bf16[128,4096]{1,0:T(8,128)(2,1)}, u32[]{:S(2)}) copy-start(bf16[128,4096]{1,0:T(8,128)(2,1)} %param.11) | copy-start | bytes 3145732
  169.8 156.6 %all-gather.5.cloned.1.call-start = ((), (), s32[]{:S(2)}) async-start(), calls=%async_computation.4 | async-start | bytes 10813440 | tf_op jit(solution)/shard_map/all_gather | solution.py:105
  171.2 62.1 %copy-start.5 = (f32[4096]{0:T(1024)S(1)}, f32[4096]{0:T(1024)}, u32[]{:S(2)}) copy-start(f32[4096]{0:T(1024)} %convert_element_type.69) | copy-start | bytes 49156
  231.3 1.9 copy-start.1
  256.8 69.6 %copy-start.9 = (bf16[1,4096,172]{1,2,0:T(8,128)(2,1)S(1)}, bf16[1,4096,172]{1,2,0:T(8,128)(2,1)}, u32[]{:S(2)}) copy-start(bf16[1,4096,172]{1,2,0:T(8,128)(2,1)} %param.14) | copy-start | bytes 4227076
  326.5 7.8 %copy-start.10 = (bf16[1,4096,172]{1,2,0:T(8,128)(2,1)S(1)}, bf16[1,4096,172]{1,2,0:T(8,128)(2,1)}, u32[]{:S(2)}) copy-start(bf16[1,4096,172]{1,2,0:T(8,128)(2,1)} %param.15) | copy-start | bytes 4227076
  326.5 15.6 %slice-start = ((s8[10485760]{0:T(1024)(128)(4,1)}), s8[4194304]{0:T(1024)(128)(4,1)S(1)}, s32[]{:S(2)}) async-start(s8[10485760]{0:T(1024)(128)(4,1)} %bitcast.52), calls=%async_computation.7 | async-start | bytes 8388608
  326.5 15.6 %slice-start.1 = ((s8[10485760]{0:T(1024)(128)(4,1)}), s8[4194304]{0:T(1024)(128)(4,1)S(1)}, s32[]{:S(2)}) async-start(s8[10485760]{0:T(1024)(128)(4,1)} %bitcast.52), calls=%async_computation.8 | async-start | bytes 8388608
  334.2 7.8 %slice-start.2 = ((s8[10485760]{0:T(1024)(128)(4,1)}), s8[2097152]{0:T(1024)(128)(4,1)S(1)}, s32[]{:S(2)}) async-start(s8[10485760]{0:T(1024)(128)(4,1)} %bitcast.52), calls=%async_computation.9 | async-start | bytes 4194304
  334.2 11.1 %slice-start.3 = ((s8[10485760]{0:T(1024)(128)(4,1)}), s8[4194304]{0:T(1024)(128)(4,1)S(1)}, s32[]{:S(2)}) async-start(s8[10485760]{0:T(1024)(128)(4,1)} %bitcast.54), calls=%async_computation.10 | async-start | bytes 8388608
  334.3 11.1 %slice-start.4 = ((s8[10485760]{0:T(1024)(128)(4,1)}), s8[4194304]{0:T(1024)(128)(4,1)S(1)}, s32[]{:S(2)}) async-start(s8[10485760]{0:T(1024)(128)(4,1)} %bitcast.54), calls=%async_computation.11 | async-start | bytes 8388608
  342.1 3.3 slice-start.5
  342.1 3.3 copy-start.11
Sparse Core Ops, SparseCore 0:
  11.2 75.3 all-reduce.2
  89.1 44.2 all-gather.8
  144.4 86.9 all-reduce.4
Sparse Core Ops, SparseCore 1:
  169.9 76.6 all-gather.6
  256.9 69.5 all-gather.4
